TPU v7x, 32 devices: a whole 2x2x4 slice. The times are simulated.
32 devices in a mesh: dp: 8 (over z, y), mp: 4 (over x, core).
Axes of the slice: x: 2, y: 2, z: 4, core: 2. Of those that a mesh axis runs over, the one named last changes fastest.
Arguments:
- tokens: bfloat16 [8192, 768], P(('dp', 'mp')), may hold values from -6 to 6
- segment_ids: int32 [8192], P('dp'), may hold values from 0 to 10, as said below
- keep_mask: int32 [88, 2], P('dp'), may hold values 0 or 1
- first_gain: bfloat16 [768], replicated, may hold values from 0.5 to 1.5
- first_shift: bfloat16 [768], replicated, may hold values from -3 to 3
- query_weight: bfloat16 [768, 768], P(None, 'mp'), may hold values from -0.21875 to 0.21875
- query_bias: bfloat16 [768], P('mp'), may hold values from -3 to 3
- key_weight: bfloat16 [768, 768], P(None, 'mp'), may hold values from -0.21875 to 0.21875
- value_weight: bfloat16 [768, 768], P(None, 'mp'), may hold values from -0.21875 to 0.21875
- value_bias: bfloat16 [768], P('mp'), may hold values from -3 to 3
- out_weight: bfloat16 [768, 768], P('mp'), may hold values from -2.5 to 2.5
- out_bias: bfloat16 [768], replicated, may hold values from -2 to 2
- second_gain: bfloat16 [768], replicated, may hold values from 0.5 to 1.5
- second_shift: bfloat16 [768], replicated, may hold values from -3 to 3
- up_weight: bfloat16 [768, 3072], P(None, 'mp'), may hold values from -0.21875 to 0.21875
- up_bias: bfloat16 [3072], P('mp'), may hold values from -3 to 3
- down_weight: bfloat16 [3072, 768], P('mp'), may hold values from -0.109375 to 0.109375
- down_bias: bfloat16 [768], replicated, may hold values from -2 to 2
- cotangent: bfloat16 [8192, 768], P(('dp', 'mp')), may hold values from -6 to 6
Outputs:
- layer_out: bfloat16 [8192, 768], P(('dp', 'mp'))
- input_grad: float32 [8192, 768], P(('dp', 'mp'))
- first_gain_grad: float32 [768], replicated
- first_shift_grad: float32 [768], replicated
- query_weight_grad: float32 [768, 768], P(None, 'mp')
- query_bias_grad: float32 [768], P('mp')
- key_weight_grad: float32 [768, 768], P(None, 'mp')
- value_weight_grad: float32 [768, 768], P(None, 'mp')
- value_bias_grad: float32 [768], P('mp')
- out_weight_grad: float32 [768, 768], P('mp')
- out_bias_grad: float32 [768], replicated
- second_gain_grad: float32 [768], replicated
- second_shift_grad: float32 [768], replicated
- up_weight_grad: float32 [768, 3072], P(None, 'mp')
- up_bias_grad: float32 [3072], P('mp')
- down_weight_grad: float32 [3072, 768], P('mp')
- down_bias_grad: float32 [768], replicated
Inputs may be any that keep to these rules, and one draw needn't show every extreme that they name: `segment_ids`: within each aligned block of 1024 tokens the ids start at 0, never fall and rise by one from image to image; every image but the last of a block has 102, 198 or 578 tokens, the last holds the remaining tokens. In the first block every image but the last has 102 tokens. `keep_mask`: row i of a block of 11 rows belongs to the image with segment id i of the same index of dp.
All inputs are finite; a program needn't handle non-finite values.
Results may differ from a plain program's by a relative error of at most 0.02.
Values may be sent and summed in bfloat16 or wider, within the bound.
No kernel may reach another device: no remote copies, remote signals or barrier semaphores. Data moves between devices by JAX's collectives and lax.ppermute only.
A program may use at most 128 MiB of HBM per device.

v0:
```python
import math
import jax
import jax.numpy as jnp
from jax import lax
from jax.sharding import PartitionSpec as P

HD = 64
eps = 1e-06


def layer_norm(values, scaling, bias_add):
    center = values - jnp.mean(values, axis=-1, keepdims=True)
    spread = jnp.mean(center * center, axis=-1, keepdims=True)
    return center * lax.rsqrt(spread + eps) * scaling + bias_add


def gelu_exact(values):
    return jax.nn.gelu(values, approximate=False)


def per_device(
    tokens,
    segment_ids,
    keep_mask,
    first_gain,
    first_shift,
    query_weight,
    query_bias,
    key_weight,
    value_weight,
    value_bias,
    out_weight,
    out_bias,
    second_gain,
    second_shift,
    up_weight,
    up_bias,
    down_weight,
    down_bias,
    cotangent,
):
    f32 = jnp.float32
    bf16 = jnp.bfloat16
    local_rows = tokens.shape[0]
    row_count = segment_ids.shape[0]
    head_width = query_weight.shape[1]
    head_group = head_width // HD
    score_scale = 1.0 / math.sqrt(HD)
    block_rows = min(512, row_count)
    block_count = row_count // block_rows
    offset = lax.axis_index("mp") * local_rows
    local_ids = lax.dynamic_slice_in_dim(segment_ids, offset, local_rows)
    onehot = (
        local_ids[:, None] == jnp.arange(keep_mask.shape[0], dtype=jnp.int32)[None, :]
    ).astype(f32)
    keep_rows = jnp.dot(onehot, keep_mask.astype(f32), precision=lax.Precision.HIGHEST) / 0.9
    allowed = segment_ids[:, None] == segment_ids[None, :]
    gain_one = first_gain.astype(f32)
    shift_one = first_shift.astype(f32)
    gain_two = second_gain.astype(f32)
    shift_two = second_shift.astype(f32)
    inputs = tokens.astype(f32)
    normed = layer_norm(inputs, gain_one, shift_one).astype(bf16)
    normed_all = lax.all_gather(normed, "mp", axis=0, tiled=True)
    query_rows = (
        jnp.dot(normed_all, query_weight, preferred_element_type=f32) + query_bias.astype(f32)
    ).astype(bf16)
    key_rows = jnp.dot(normed_all, key_weight, preferred_element_type=f32).astype(bf16)
    value_rows = (
        jnp.dot(normed_all, value_weight, preferred_element_type=f32) + value_bias.astype(f32)
    ).astype(bf16)
    key_heads = key_rows.reshape(row_count, head_group, HD)
    value_heads = value_rows.reshape(row_count, head_group, HD)
    context_parts = []
    lse_parts = []
    for number in range(block_count):
        row_start = number * block_rows
        query_block = query_rows[row_start : row_start + block_rows].reshape(
            block_rows, head_group, HD
        )
        scores = (
            jnp.einsum("qhd,khd->hqk", query_block, key_heads, preferred_element_type=f32)
            * score_scale
        )
        scores = jnp.where(allowed[row_start : row_start + block_rows][None], scores, -1e30)
        largest = jnp.max(scores, axis=-1, keepdims=True)
        powers = jnp.exp(scores - largest)
        totals = jnp.sum(powers, axis=-1, keepdims=True)
        weights = (powers / totals).astype(bf16)
        context_block = jnp.einsum("hqk,khd->qhd", weights, value_heads, preferred_element_type=f32)
        context_parts.append(context_block.reshape(block_rows, head_width))
        lse_parts.append(largest + jnp.log(totals))
    context = jnp.concatenate(context_parts, axis=0).astype(bf16)
    attended = lax.psum_scatter(
        jnp.dot(context, out_weight, preferred_element_type=f32).astype(jnp.bfloat16),
        "mp",
        scatter_dimension=0,
        tiled=True,
    ).astype(jnp.float32) + out_bias.astype(f32)
    middle = inputs + keep_rows[:, 0:1] * attended
    normed_two = layer_norm(middle, gain_two, shift_two).astype(bf16)
    normed_two_all = lax.all_gather(normed_two, "mp", axis=0, tiled=True)
    hidden = jnp.dot(normed_two_all, up_weight, preferred_element_type=f32) + up_bias.astype(f32)
    activated = gelu_exact(hidden).astype(bf16)
    mlp_out = lax.psum_scatter(
        jnp.dot(activated, down_weight, preferred_element_type=f32).astype(jnp.bfloat16),
        "mp",
        scatter_dimension=0,
        tiled=True,
    ).astype(jnp.float32) + down_bias.astype(f32)
    layer_out = (middle + keep_rows[:, 1:2] * mlp_out).astype(bf16)
    out_grad = cotangent.astype(f32)
    mlp_grad = out_grad * keep_rows[:, 1:2]
    down_bias_grad = jnp.sum(mlp_grad, axis=0)
    mlp_grad_all = lax.all_gather(mlp_grad.astype(bf16), "mp", axis=0, tiled=True)
    down_weight_grad = jnp.einsum("rf,rd->fd", activated, mlp_grad_all, preferred_element_type=f32)
    act_grad = jnp.einsum("rd,fd->rf", mlp_grad_all, down_weight, preferred_element_type=f32)
    unused_value, gelu_pull = jax.vjp(gelu_exact, hidden)
    hidden_grad = gelu_pull(act_grad)[0].astype(bf16)
    up_bias_grad = jnp.sum(hidden_grad.astype(f32), axis=0)
    up_weight_grad = jnp.einsum(
        "rd,rf->df", normed_two_all, hidden_grad, preferred_element_type=f32
    )
    second_grad = lax.psum_scatter(
        jnp.einsum("rf,df->rd", hidden_grad, up_weight, preferred_element_type=f32).astype(
            jnp.bfloat16
        ),
        "mp",
        scatter_dimension=0,
        tiled=True,
    ).astype(jnp.float32)
    unused_value, norm_pull_two = jax.vjp(layer_norm, middle, gain_two, shift_two)
    middle_part, gain_two_grad, shift_two_grad = norm_pull_two(second_grad)
    middle_grad = out_grad + middle_part
    attn_grad = middle_grad * keep_rows[:, 0:1]
    out_bias_grad = jnp.sum(attn_grad, axis=0)
    attn_grad_all = lax.all_gather(attn_grad.astype(bf16), "mp", axis=0, tiled=True)
    out_weight_grad = jnp.einsum("rc,rd->cd", context, attn_grad_all, preferred_element_type=f32)
    context_grad = jnp.einsum(
        "rd,cd->rc", attn_grad_all, out_weight, preferred_element_type=f32
    ).astype(bf16)
    context_grad_heads = context_grad.reshape(row_count, head_group, HD)
    query_grads = []
    key_grad = jnp.zeros((row_count, head_group, HD), f32)
    value_grad = jnp.zeros((row_count, head_group, HD), f32)
    for number in range(block_count):
        row_start = number * block_rows
        query_block = query_rows[row_start : row_start + block_rows].reshape(
            block_rows, head_group, HD
        )
        scores = (
            jnp.einsum("qhd,khd->hqk", query_block, key_heads, preferred_element_type=f32)
            * score_scale
        )
        scores = jnp.where(allowed[row_start : row_start + block_rows][None], scores, -1e30)
        probs = jnp.exp(scores - lse_parts[number])
        grad_block = context_grad_heads[row_start : row_start + block_rows]
        prob_grad = jnp.einsum("qhd,khd->hqk", grad_block, value_heads, preferred_element_type=f32)
        center = jnp.sum(probs * prob_grad, axis=-1, keepdims=True)
        score_grad = (probs * (prob_grad - center)).astype(bf16)
        query_grads.append(
            jnp.einsum("hqk,khd->qhd", score_grad, key_heads, preferred_element_type=f32)
            * score_scale
        )
        key_grad = (
            key_grad
            + jnp.einsum("hqk,qhd->khd", score_grad, query_block, preferred_element_type=f32)
            * score_scale
        )
        value_grad = value_grad + jnp.einsum(
            "hqk,qhd->khd", probs.astype(bf16), grad_block, preferred_element_type=f32
        )
    query_grad_rows = (
        jnp.concatenate(query_grads, axis=0).reshape(row_count, head_width).astype(bf16)
    )
    key_grad_rows = key_grad.reshape(row_count, head_width).astype(bf16)
    value_grad_rows = value_grad.reshape(row_count, head_width).astype(bf16)
    query_bias_grad = jnp.sum(query_grad_rows.astype(f32), axis=0)
    value_bias_grad = jnp.sum(value_grad_rows.astype(f32), axis=0)
    query_weight_grad = jnp.einsum(
        "rd,rc->dc", normed_all, query_grad_rows, preferred_element_type=f32
    )
    key_weight_grad = jnp.einsum("rd,rc->dc", normed_all, key_grad_rows, preferred_element_type=f32)
    value_weight_grad = jnp.einsum(
        "rd,rc->dc", normed_all, value_grad_rows, preferred_element_type=f32
    )
    total = jnp.einsum("rc,dc->rd", query_grad_rows, query_weight, preferred_element_type=f32)
    total = total + jnp.einsum("rc,dc->rd", key_grad_rows, key_weight, preferred_element_type=f32)
    first_grad = lax.psum_scatter(
        (
            total
            + jnp.einsum("rc,dc->rd", value_grad_rows, value_weight, preferred_element_type=f32)
        ).astype(jnp.bfloat16),
        "mp",
        scatter_dimension=0,
        tiled=True,
    ).astype(jnp.float32)
    unused_value, norm_pull_one = jax.vjp(layer_norm, inputs, gain_one, shift_one)
    input_part, gain_one_grad, shift_one_grad = norm_pull_one(first_grad)
    input_grad = middle_grad + input_part
    (
        query_weight_grad,
        query_bias_grad,
        key_weight_grad,
        value_weight_grad,
        value_bias_grad,
        out_weight_grad,
        up_weight_grad,
        up_bias_grad,
        down_weight_grad,
    ) = lax.psum(
        (
            query_weight_grad,
            query_bias_grad,
            key_weight_grad,
            value_weight_grad,
            value_bias_grad,
            out_weight_grad,
            up_weight_grad,
            up_bias_grad,
            down_weight_grad,
        ),
        "dp",
    )
    gain_one_grad, shift_one_grad, out_bias_grad, gain_two_grad, shift_two_grad, down_bias_grad = (
        lax.psum(
            (
                gain_one_grad,
                shift_one_grad,
                out_bias_grad,
                gain_two_grad,
                shift_two_grad,
                down_bias_grad,
            ),
            ("dp", "mp"),
        )
    )
    return (
        layer_out,
        input_grad,
        gain_one_grad,
        shift_one_grad,
        query_weight_grad,
        query_bias_grad,
        key_weight_grad,
        value_weight_grad,
        value_bias_grad,
        out_weight_grad,
        out_bias_grad,
        gain_two_grad,
        shift_two_grad,
        up_weight_grad,
        up_bias_grad,
        down_weight_grad,
        down_bias_grad,
    )


def solution(mesh):
    in_specs = (
        P(("dp", "mp"), None),
        P("dp"),
        P("dp", None),
        P(),
        P(),
        P(None, "mp"),
        P("mp"),
        P(None, "mp"),
        P(None, "mp"),
        P("mp"),
        P("mp", None),
        P(),
        P(),
        P(),
        P(None, "mp"),
        P("mp"),
        P("mp", None),
        P(),
        P(("dp", "mp"), None),
    )
    out_specs = (
        P(("dp", "mp"), None),
        P(("dp", "mp"), None),
        P(),
        P(),
        P(None, "mp"),
        P("mp"),
        P(None, "mp"),
        P(None, "mp"),
        P("mp"),
        P("mp", None),
        P(),
        P(),
        P(),
        P(None, "mp"),
        P("mp"),
        P("mp", None),
        P(),
    )
    return jax.shard_map(
        per_device, mesh=mesh, in_specs=in_specs, out_specs=out_specs, check_vma=False
    )
```

profile of v0, /device:TPU:0, one launch (start us, length us, event | category | flops | bytes accessed | tf_op | source)
XLA Modules:
  0.0 535.1 jit_solution(10001136210454369403)
XLA Ops:
  7.3 1.2 convert_reduce_fusion.3
  8.5 1.2 fusion.45
  11.7 2.0 fusion.43
  15.1 1.4 broadcast_compare_fusion
  17.6 18.7 %all-gather.5.cloned.1.call-done = bf16[1024,768]{1,0:T(8,128)(2,1)} async-done(((bf16[256,768]{1,0:T(8,128)(2,1)}), bf16[1024,768]{1,0:T(8,128)(2,1)}) %all-gather.5.cloned.1.call-update) | async-done | bytes 1572880 | tf_op jit(solution)/shard_map/all_gather | solution.py:64
  36.2 2.3 fusion.27
  39.3 1.4 fusion.65
  40.7 1.5 fusion
  43.3 1.6 fusion.35
  45.0 1.4 fusion.64
  46.5 1.5 fusion.1
  48.0 1.1 copy-done.3
  49.7 1.7 fusion.34
  52.0 1.8 convolution_convert_fusion.2
  55.3 1.3 convert_element_type.168
  58.1 23.9 %reduce-scatter.5.cloned.1.call-done = bf16[256,768]{1,0:T(8,128)(2,1)} async-done(((bf16[1024,768]{1,0:T(8,128)(2,1)}), bf16[256,768]{1,0:T(8,128)(2,1)}) %reduce-scatter.5.cloned.1.call-update) | async-done | bytes 393232 | tf_op jit(solution)/shard_map/reduce_scatter | solution.py:94
  82.0 1.3 fusion.57
  83.3 1.3 multiply_reduce_fusion.2
  85.9 2.0 add_convert_fusion.3
  88.0 1.6 fusion.37
  90.8 16.9 %all-gather.7.cloned.1.call-done = bf16[1024,768]{1,0:T(8,128)(2,1)} async-done(((bf16[256,768]{1,0:T(8,128)(2,1)}), bf16[1024,768]{1,0:T(8,128)(2,1)}) %all-gather.7.cloned.1.call-update) | async-done | bytes 1572880 | tf_op jit(solution)/shard_map/all_gather | solution.py:102
  107.7 4.8 fusion.66
  112.5 16.9 %all-gather.9.cloned.1.call-done = bf16[1024,768]{1,0:T(8,128)(2,1)} async-done(((bf16[256,768]{1,0:T(8,128)(2,1)}), bf16[1024,768]{1,0:T(8,128)(2,1)}) %all-gather.9.cloned.1.call-update) | async-done | bytes 1572880 | tf_op jit(solution)/shard_map/all_gather | solution.py:115
  129.4 11.8 %convert_reduce_fusion = (f32[768]{0:T(1024)}, bf16[1024,768]{1,0:T(8,128)(2,1)S(1)}, f32[1024,768]{1,0:T(8,128)}) fusion(f32[1024,768]{1,0:T(8,128)} %fusion.66, f32[768]{0:T(1024)S(1)} %convert_element_type.170, bf16[1024,768]{1,0:T(8,128)(2,1)} %all-gather.9.cloned.1.call-done, bf16[768,768]{1,0:T(8,128)(2,1)S(1)} %copy-done), kind=kOutput, calls=%fused_computation.20 | convolution fusion | flops 1266941184 | bytes 10622976 | tf_op jit(solution)/shard_map/rd,fd->rf/dot_general | solution.py:117
  141.2 1.2 copy-done.62
  142.4 2.6 convolution_convert_fusion
  145.0 3.3 multiply_convert_fusion.2
  148.3 1.1 copy-done.24
  149.5 2.5 convolution_convert_fusion.1
  152.1 1.4 convert_element_type.174
  153.5 19.7 %reduce-scatter.9.cloned.1.call-done = bf16[256,768]{1,0:T(8,128)(2,1)} async-done(((bf16[1024,768]{1,0:T(8,128)(2,1)}), bf16[256,768]{1,0:T(8,128)(2,1)}) %reduce-scatter.9.cloned.1.call-update) | async-done | bytes 393232 | tf_op jit(solution)/shard_map/reduce_scatter | solution.py:124
  173.1 2.1 fusion.47
  175.2 1.2 multiply_multiply_fusion.6
  176.5 27.7 %reduce-scatter.7.cloned.1.call-done = bf16[256,768]{1,0:T(8,128)(2,1)} async-done(((bf16[1024,768]{1,0:T(8,128)(2,1)}), bf16[256,768]{1,0:T(8,128)(2,1)}) %reduce-scatter.7.cloned.1.call-update) | async-done | bytes 393232 | tf_op jit(solution)/shard_map/reduce_scatter | solution.py:105
  204.2 2.6 fusion.59
  206.8 2.4 fusion.36
  210.8 18.1 %all-gather.11.cloned.1.call-done = bf16[1024,768]{1,0:T(8,128)(2,1)} async-done(((bf16[256,768]{1,0:T(8,128)(2,1)}), bf16[1024,768]{1,0:T(8,128)(2,1)}) %all-gather.11.cloned.1.call-update) | async-done | bytes 1572880 | tf_op jit(solution)/shard_map/all_gather | solution.py:137
  229.0 2.1 convolution_convert_fusion.3
  231.1 3.9 multiply_reduce_fusion.1
  235.8 1.4 multiply_convert_fusion.1
  237.2 1.1 fusion.29
  239.0 1.2 fusion.5
  240.2 1.9 multiply_reduce_fusion
  242.1 1.8 convert_reduce_fusion.4
  244.0 1.4 multiply_convert_fusion
  245.4 1.1 fusion.28
  249.6 1.8 add_convert_fusion
  251.7 4.9 fusion.71
  256.6 2.8 fusion.70
  259.5 1.3 fusion.50
  260.8 1.3 fusion.74
  262.1 1.3 fusion.72
  263.4 1.3 fusion.73
  265.5 22.2 %all-reduce.1 = (f32[192]{0:T(256)}, f32[192]{0:T(256)}, f32[768]{0:T(1024)}) all-reduce(f32[192]{0:T(256)S(1)} %reduce_sum.217, f32[192]{0:T(256)S(1)} %reduce_sum.219, f32[768]{0:T(1024)S(1)} %copy-done.58), channel_id=1, replica_groups=mesh['dp'=8,'mp'=4] {'dp'}, use_global_device_ids=true, to_apply=%region_24.25 | all-reduce | flops 1152 | bytes 9216 | tf_op jit(solution)/shard_map/psum | solution.py:211
  287.7 1.3 convert_reduce_fusion.1
  289.0 1.5 fusion.48
  290.6 41.8 %all-reduce = (f32[768]{0:T(1024)}, f32[768]{0:T(1024)}, f32[768]{0:T(1024)}, f32[768]{0:T(1024)}, f32[768]{0:T(1024)}, /*index=5*/f32[768]{0:T(1024)}) all-reduce(f32[768]{0:T(1024)S(1)} %get-tuple-element.19, f32[768]{0:T(1024)S(1)} %get-tuple-element.24, f32[768]{0:T(1024)S(1)} %copy-done.50, ...), channel_id=1, replica_groups=mesh['dp'=8,'mp'=4] {'dp','mp'}, use_global_device_ids=true, to_apply=%region_19.20 | all-reduce | flops 4608 | bytes 36864 | tf_op jit(solution)/shard_map/psum | solution.py:226
  332.3 2.3 add_add_fusion.2
  334.6 184.2 %all-reduce.5.cloned.1.call-done = (f32[768,192]{0,1:T(8,128)}, f32[768,192]{0,1:T(8,128)}, f32[768,192]{0,1:T(8,128)}, f32[192,768]{1,0:T(8,128)}, f32[768,768]{1,0:T(8,128)}, /*index=5*/f32[768,768]{1,0:T(8,128)}) async-done(((f32[768,192]{0,1:T(8,128)}, f32[768,192]{0,1:T(8,128)}, f32[768,192]{0,1:T(8,128)}, f32[192,768]{1,0:T(8,128)}, f32[768,768]{1,0:T(8,128)}, /*index=5*/f32[768,768]{1,0:T(8,128)}), ...) | async-done | bytes 7077904 | tf_op jit(solution)/shard_map/psum | solution.py:211
  518.8 2.1 copy.42
  520.9 1.9 copy.43
  522.8 1.9 copy.44
  525.6 1.4 copy.46
  527.0 1.4 copy.47
  (186 shorter events, 21.3 us)
Async XLA Ops:
  7.2 122.2 %copy-start = (bf16[768,768]{1,0:T(8,128)(2,1)S(1)}, bf16[768,768]{1,0:T(8,128)(2,1)}, u32[]{:S(2)}) copy-start(bf16[768,768]{1,0:T(8,128)(2,1)} %param.35) | copy-start | bytes 3538948
  7.2 29.0 %all-gather.5.cloned.1.call-start = ((), (), s32[]{:S(2)}) async-start(), calls=%async_computation.4 | async-start | bytes 1966080 | tf_op jit(solution)/shard_map/all_gather | solution.py:64
  8.5 6.0 %copy-start.40 = (f32[256]{0:T(256)}, f32[256]{0:T(256)S(1)}, u32[]{:S(2)}) copy-start(f32[256]{0:T(256)S(1)} %broadcast_multiply_fusion.1) | copy-start | bytes 3076
  10.3 4.1 copy-start.45
  11.0 3.4 copy-start.37
  13.7 68.3 %reduce-scatter.5.cloned.1.call-start = ((), (), s32[]{:S(2)}) async-start(), calls=%async_computation.5 | async-start | bytes 1966080 | tf_op jit(solution)/shard_map/reduce_scatter | solution.py:94
  15.1 23.4 %copy-start.34 = (bf16[768,192]{0,1:T(8,128)(2,1)S(1)}, bf16[768,192]{0,1:T(8,128)(2,1)}, u32[]{:S(2)}) copy-start(bf16[768,192]{0,1:T(8,128)(2,1)} %param.26) | copy-start | bytes 884740
  36.2 2.3 copy-start.5
  36.2 3.0 copy-start.19
  38.5 2.1 copy-start.20
  38.6 6.5 %copy-start.16 = (bf16[512,192]{0,1:T(8,128)(2,1)}, bf16[512,192]{0,1:T(8,128)(2,1)S(1)}, u32[]{:S(2)}) copy-start(bf16[512,192]{0,1:T(8,128)(2,1)S(1)} %get-tuple-element.55) | copy-start | bytes 589828
  39.2 5.8 %copy-start.7 = (bf16[1024,192]{0,1:T(8,128)(2,1)}, bf16[1024,192]{0,1:T(8,128)(2,1)S(1)}, u32[]{:S(2)}) copy-start(bf16[1024,192]{0,1:T(8,128)(2,1)S(1)} %convolution_convert_fusion.4) | copy-start | bytes 1179652
  40.7 2.6 copy-start.2
  40.7 1.5 copy-start.32
  42.2 2.8 copy-start.42
  42.9 5.1 copy-start.22
  43.3 1.7 copy-start.18
  45.0 6.4 %copy-start.26 = (bf16[3,64,512]{2,1,0:T(8,128)(2,1)}, bf16[3,64,512]{2,1,0:T(8,128)(2,1)S(1)}, u32[]{:S(2)}) copy-start(bf16[3,64,512]{2,1,0:T(8,128)(2,1)S(1)} %fusion.35) | copy-start | bytes 589828
  46.5 2.6 copy-start.3
  46.5 2.6 copy-start.39
  49.7 2.3 copy-start.31
  51.4 3.3 copy-start.59
  51.4 30.7 %copy-start.4 = (bf16[256,768]{1,0:T(8,128)(2,1)S(1)}, bf16[256,768]{1,0:T(8,128)(2,1)}, u32[]{:S(2)}) copy-start(bf16[256,768]{1,0:T(8,128)(2,1)} %param.19) | copy-start | bytes 1179652
  52.0 35.9 %copy-start.11 = (bf16[256,768]{1,0:T(8,128)(2,1)S(1)}, bf16[256,768]{1,0:T(8,128)(2,1)}, u32[]{:S(2)}) copy-start(bf16[256,768]{1,0:T(8,128)(2,1)} %param.37) | copy-start | bytes 1179652
  53.8 53.9 %all-gather.7.cloned.1.call-start = ((), (), s32[]{:S(2)}) async-start(), calls=%async_computation.6 | async-start | bytes 1966080 | tf_op jit(solution)/shard_map/all_gather | solution.py:102
  83.3 2.0 copy-start.44
  87.9 41.4 %all-gather.9.cloned.1.call-start = ((), (), s32[]{:S(2)}) async-start(), calls=%async_computation.8 | async-start | bytes 1966080 | tf_op jit(solution)/shard_map/all_gather | solution.py:115
  89.6 83.6 %reduce-scatter.9.cloned.1.call-start = ((), (), s32[]{:S(2)}) async-start(), calls=%async_computation.9 | async-start | bytes 1966080 | tf_op jit(solution)/shard_map/reduce_scatter | solution.py:124
  129.4 13.0 %copy-start.61 = (bf16[768,768]{1,0:T(8,128)(2,1)S(1)}, bf16[768,768]{1,0:T(8,128)(2,1)}, u32[]{:S(2)}) copy-start(bf16[768,768]{1,0:T(8,128)(2,1)} %param.33) | copy-start | bytes 3538948
  145.0 59.2 %reduce-scatter.7.cloned.1.call-start = ((), (), s32[]{:S(2)}) async-start(), calls=%async_computation.7 | async-start | bytes 1966080 | tf_op jit(solution)/shard_map/reduce_scatter | solution.py:105
  149.5 23.7 %copy-start.6 = (bf16[256,768]{1,0:T(8,128)(2,1)S(1)}, bf16[256,768]{1,0:T(8,128)(2,1)}, u32[]{:S(2)}) copy-start(bf16[256,768]{1,0:T(8,128)(2,1)} %reduce-scatter.5.cloned.1.call-done) | copy-start | bytes 1179652
  152.0 54.8 %copy-start.12 = (bf16[256,768]{1,0:T(8,128)(2,1)S(1)}, bf16[256,768]{1,0:T(8,128)(2,1)}, u32[]{:S(2)}) copy-start(bf16[256,768]{1,0:T(8,128)(2,1)} %param.37) | copy-start | bytes 1179652
  152.0 76.9 %all-gather.11.cloned.1.call-start = ((), (), s32[]{:S(2)}) async-start(), calls=%async_computation.10 | async-start | bytes 1966080 | tf_op jit(solution)/shard_map/all_gather | solution.py:137
  206.8 24.3 %copy-start.23 = (bf16[1024,192]{0,1:T(8,128)(2,1)S(1)}, bf16[1024,192]{0,1:T(8,128)(2,1)}, u32[]{:S(2)}) copy-start(bf16[1024,192]{0,1:T(8,128)(2,1)} %copy-done.22) | copy-start | bytes 1179652
  206.8 2.4 copy-start.52
  209.2 78.5 %reduce-scatter.11.cloned.1.call-start = ((), (), s32[]{:S(2)}) async-start(), calls=%async_computation.11 | async-start | bytes 1966080 | tf_op jit(solution)/shard_map/reduce_scatter | solution.py:189
  231.1 4.0 slice-start
  231.1 4.7 slice-start.1
  235.1 3.9 slice-start.2
  235.8 1.4 copy-start.8
  235.8 3.2 slice-start.3
  247.1 1.8 copy-start.36
  248.0 1.5 copy-start.33
  251.4 267.4 %all-reduce.5.cloned.1.call-start = ((), (), s32[]{:S(2)}) async-start(), calls=%async_computation.12 | async-start | bytes 14155776 | tf_op jit(solution)/shard_map/psum | solution.py:211
  251.7 4.9 copy-start.60
  251.7 4.9 copy-start.63
  256.6 2.9 copy-start.25
  256.6 2.9 copy-start.27
  256.6 2.9 copy-start.29
  259.5 2.6 copy-start.10
  264.7 23.0 %copy-start.38 = (f32[768]{0:T(1024)S(1)}, f32[768]{0:T(1024)}, u32[]{:S(2)}) copy-start(f32[768]{0:T(1024)} %copy-done.37) | copy-start | bytes 9220
  264.7 23.0 %copy-start.41 = (f32[256]{0:T(256)S(1)}, f32[256]{0:T(256)}, u32[]{:S(2)}) copy-start(f32[256]{0:T(256)} %copy-done.40) | copy-start | bytes 3076
  264.7 24.3 %copy-start.55 = (f32[256]{0:T(256)S(1)}, f32[256]{0:T(256)}, u32[]{:S(2)}) copy-start(f32[256]{0:T(256)} %copy-done.54) | copy-start | bytes 3076
  264.7 24.3 %copy-start.46 = (f32[256]{0:T(256)S(1)}, f32[256]{0:T(256)}, u32[]{:S(2)}) copy-start(f32[256]{0:T(256)} %copy-done.45) | copy-start | bytes 3076
  264.7 25.8 %copy-start.47 = (f32[768]{0:T(1024)S(1)}, f32[768]{0:T(1024)}, u32[]{:S(2)}) copy-start(f32[768]{0:T(1024)} %get-tuple-element.17) | copy-start | bytes 9220
  264.7 25.8 %copy-start.48 = (f32[768]{0:T(1024)S(1)}, f32[768]{0:T(1024)}, u32[]{:S(2)}) copy-start(f32[768]{0:T(1024)} %get-tuple-element.23) | copy-start | bytes 9220
  264.7 25.8 %copy-start.49 = (f32[768]{0:T(1024)S(1)}, f32[768]{0:T(1024)}, u32[]{:S(2)}) copy-start(f32[768]{0:T(1024)} %get-tuple-element.21) | copy-start | bytes 9220
  264.7 25.8 %copy-start.50 = (f32[768]{0:T(1024)S(1)}, f32[768]{0:T(1024)}, u32[]{:S(2)}) copy-start(f32[768]{0:T(1024)} %get-tuple-element.22) | copy-start | bytes 9220
  264.7 67.6 %copy-start.13 = (bf16[256,768]{1,0:T(8,128)(2,1)S(1)}, bf16[256,768]{1,0:T(8,128)(2,1)}, u32[]{:S(2)}) copy-start(bf16[256,768]{1,0:T(8,128)(2,1)} %param.37) | copy-start | bytes 1179652
  264.8 67.6 %copy-start.53 = (f32[256]{0:T(256)S(1)}, f32[256]{0:T(256)}, u32[]{:S(2)}) copy-start(f32[256]{0:T(256)} %copy-done.52) | copy-start | bytes 3076
  518.8 5.9 %copy-start.30 = (f32[192,768]{1,0:T(8,128)S(1)}, f32[192,768]{1,0:T(8,128)}, u32[]{:S(2)}) copy-start(f32[192,768]{1,0:T(8,128)} %get-tuple-element.77) | copy-start | bytes 1769476
  518.8 6.7 %copy-start.15 = (f32[768,768]{1,0:T(8,128)S(1)}, f32[768,768]{1,0:T(8,128)}, u32[]{:S(2)}) copy-start(f32[768,768]{1,0:T(8,128)} %get-tuple-element.81) | copy-start | bytes 7077892
  524.7 2.2 copy-start.14
  525.6 2.8 copy-start.1
  (13 other events, 10.8 us)
Sparse Core Ops, SparseCore 0:
  13.8 22.3 all-gather.4
  54.0 28.0 reduce-scatter.4
  88.0 19.6 all-gather.6
  109.7 19.6 all-gather.8
  145.1 27.9 reduce-scatter.8
  176.1 28.0 reduce-scatter.6
  209.3 19.6 all-gather.10
  251.6 27.9 reduce-scatter.10
  285.8 232.9 all-reduce.4
where the time goes:
time: 544 us; the launch traced here: 535 us
  waiting for transfers between devices  326 us (60%)
  matrix products  64.6 us (12%)
  blocking collectives  63.9 us (12%)
  other arithmetic  42.8 us (8%)
  local copies, waits for them, and re-layouts  21.6 us (4%)
  between operations  14.8 us (3%)
    psum x1, waiting for transfers between devices, per_device(): lax.psum((query_weight_grad, query_bias_grad, key_weight_grad, value_weig...  184 us
    psum x1, blocking collectives, per_device(): lax.psum((gain_one_grad, shift_one_grad, out_bias_grad, gain_two_grad, sh...  41.8 us
    reduce_scatter x1, waiting for transfers between devices, per_device(): lax.psum_scatter(jnp.dot(activated, down_weight, preferred_element_type=f...  27.7 us
    reduce_scatter x1, waiting for transfers between devices, per_device(): lax.psum_scatter(jnp.dot(context, out_weight, preferred_element_type=f32)...  23.9 us
    psum x1, blocking collectives, per_device(): lax.psum((query_weight_grad, query_bias_grad, key_weight_grad, value_weig...  22.2 us
    reduce_scatter x1, waiting for transfers between devices, per_device(): lax.psum_scatter(jnp.einsum('rf,df->rd', hidden_grad, up_weight, preferre...  19.7 us
    unnamed x142, local copies, waits for them, and re-layouts  18.9 us
    all_gather x1, waiting for transfers between devices, per_device(): normed_all = lax.all_gather(normed, 'mp', axis=0, tiled=True)  18.7 us
  transfers between devices with their start and end apart: 9, of which 8 were waited for; matrix products, arithmetic and copies ran while one was open for 8% of the time, Pallas kernels for 0%

commit v1 on v0

--- a/solution.py
+++ b/solution.py
@@ -112,7 +112,24 @@
     out_grad = cotangent.astype(f32)
     mlp_grad = out_grad * keep_rows[:, 1:2]
     down_bias_grad = jnp.sum(mlp_grad, axis=0)
-    mlp_grad_all = lax.all_gather(mlp_grad.astype(bf16), "mp", axis=0, tiled=True)
+    value = mlp_grad.astype(bf16)
+    size, index, span = (lax.axis_size("mp"), lax.axis_index("mp"), value.shape[0])
+    right = [(i, (i + 1) % size) for i in range(size)]
+    left = [(i, (i - 1) % size) for i in range(size)]
+    mlp_grad_all = jnp.zeros((*value.shape[:0], size * span, *value.shape[0 + 1 :]), value.dtype)
+    mlp_grad_all = lax.dynamic_update_slice_in_dim(mlp_grad_all, value, index * span, axis=0)
+    from_left = from_right = value
+    halfway = size // 2
+    for step in range(1, halfway + 1):
+        from_left = lax.ppermute(from_left, "mp", right)
+        mlp_grad_all = lax.dynamic_update_slice_in_dim(
+            mlp_grad_all, from_left, (index - step) % size * span, axis=0
+        )
+        if step < size - halfway:
+            from_right = lax.ppermute(from_right, "mp", left)
+            mlp_grad_all = lax.dynamic_update_slice_in_dim(
+                mlp_grad_all, from_right, (index + step) % size * span, axis=0
+            )
     down_weight_grad = jnp.einsum("rf,rd->fd", activated, mlp_grad_all, preferred_element_type=f32)
     act_grad = jnp.einsum("rd,fd->rf", mlp_grad_all, down_weight, preferred_element_type=f32)
     unused_value, gelu_pull = jax.vjp(gelu_exact, hidden)

time: 544 us -> 525 us (0.965); the launches traced: 535 us -> 524 us
  waiting for transfers between devices: 326 us -> 311 us
  local copies, waits for them, and re-layouts: 21.6 us -> 27.1 us
    ppermute x0 -> x3, waiting for transfers between devices: none -> 18.8 us  [the longest x2 18.6 us: per_device(): from_left = lax.ppermute(from_left, 'mp', right)]
    all_gather x1, waiting for transfers between devices: 16.9 us -> 0.01 us  [per_device(): normed_two_all = lax.all_gather(normed_two, 'mp', axis=0, tiled=True)]
    all_gather x1 -> x0, waiting for transfers between devices: 16.9 us -> none  [per_device(): lax.all_gather(mlp_grad.astype(bf16), 'mp', axis=0, tiled=True)]
    unnamed x142 -> x150, local copies, waits for them, and re-layouts: 18.9 us -> 20 us
  transfers between devices with their start and end apart: 9 -> 11, of which waited for: 8 -> 9; matrix products, arithmetic and copies ran while one was open for 8% -> 9% of each run, Pallas kernels for 0% -> 0%
where the time goes in v1:
time: 525 us; the launch traced here: 524 us
  waiting for transfers between devices  311 us (59%)
  blocking collectives  63.9 us (12%)
  matrix products  61.5 us (12%)
  other arithmetic  43.4 us (8%)
  local copies, waits for them, and re-layouts  27.1 us (5%)
  between operations  15 us (3%)
    psum x1, waiting for transfers between devices, per_device(): lax.psum((query_weight_grad, query_bias_grad, key_weight_grad, value_weig...  184 us
    psum x1, blocking collectives, per_device(): lax.psum((gain_one_grad, shift_one_grad, out_bias_grad, gain_two_grad, sh...  41.7 us
    reduce_scatter x1, waiting for transfers between devices, per_device(): lax.psum_scatter(jnp.dot(activated, down_weight, preferred_element_type=f...  27.1 us
    reduce_scatter x1, waiting for transfers between devices, per_device(): lax.psum_scatter(jnp.dot(context, out_weight, preferred_element_type=f32)...  23.8 us
    psum x1, blocking collectives, per_device(): lax.psum((query_weight_grad, query_bias_grad, key_weight_grad, value_weig...  22.2 us
    unnamed x150, local copies, waits for them, and re-layouts  20 us
    reduce_scatter x1, waiting for transfers between devices, per_device(): lax.psum_scatter(jnp.einsum('rf,df->rd', hidden_grad, up_weight, preferre...  19.7 us
    all_gather x1, waiting for transfers between devices, per_device(): normed_all = lax.all_gather(normed, 'mp', axis=0, tiled=True)  18.7 us
  transfers between devices with their start and end apart: 11, of which 9 were waited for; matrix products, arithmetic and copies ran while one was open for 9% of the time, Pallas kernels for 0%

profile of v1, /device:TPU:0, one launch (start us, length us, event | category | flops | bytes accessed | tf_op | source)
XLA Modules:
  0.0 523.9 jit_solution(11726729894433210002)
XLA Ops:
  7.3 1.2 convert_reduce_fusion.3
  8.5 1.2 fusion.45
  11.7 2.0 fusion.43
  15.1 1.4 broadcast_compare_fusion
  17.5 18.7 %all-gather.4.cloned.1.call-done = bf16[1024,768]{1,0:T(8,128)(2,1)} async-done(((bf16[256,768]{1,0:T(8,128)(2,1)}), bf16[1024,768]{1,0:T(8,128)(2,1)}) %all-gather.4.cloned.1.call-update) | async-done | bytes 1572880 | tf_op jit(solution)/shard_map/all_gather | solution.py:64
  36.2 2.3 fusion.27
  39.2 1.4 fusion.66
  40.7 1.5 fusion
  43.3 1.6 fusion.35
  45.0 1.4 fusion.65
  46.5 1.5 fusion.1
  49.7 1.6 fusion.34
  52.0 1.8 convolution_convert_fusion.2
  55.3 1.3 convert_element_type.168
  58.1 23.8 %reduce-scatter.5.cloned.1.call-done = bf16[256,768]{1,0:T(8,128)(2,1)} async-done(((bf16[1024,768]{1,0:T(8,128)(2,1)}), bf16[256,768]{1,0:T(8,128)(2,1)}) %reduce-scatter.5.cloned.1.call-update) | async-done | bytes 393232 | tf_op jit(solution)/shard_map/reduce_scatter | solution.py:94
  82.0 1.3 fusion.57
  83.2 1.3 multiply_reduce_fusion.2
  85.7 2.0 add_convert_fusion.3
  88.0 1.6 constant_dynamic-update-slice_fusion.3
  90.7 1.7 collective-permute-start.1
  92.4 13.2 %collective-permute-done = bf16[256,768]{1,0:T(8,128)(2,1)S(1)} collective-permute-done((bf16[256,768]{1,0:T(8,128)(2,1)}, bf16[256,768]{1,0:T(8,128)(2,1)S(1)}, u32[]{:S(2)}, u32[]{:S(2)}) %collective-permute-start) | collective-permute-done | bytes 393248 | tf_op jit(solution)/shard_map/ppermute | solution.py:124
  105.6 1.3 convert_element_type.170
  107.9 1.8 constant_dynamic-update-slice_fusion.1
  109.6 5.4 %collective-permute-done.2 = bf16[256,768]{1,0:T(8,128)(2,1)} collective-permute-done((bf16[256,768]{1,0:T(8,128)(2,1)S(1)}, bf16[256,768]{1,0:T(8,128)(2,1)}, u32[]{:S(2)}, u32[]{:S(2)}) %collective-permute-start.2) | collective-permute-done | bytes 393248 | tf_op jit(solution)/shard_map/ppermute | solution.py:124
  115.0 1.8 constant_dynamic-update-slice_fusion
  116.8 3.3 fusion.67
  120.1 10.3 %convert_reduce_fusion = (f32[768]{0:T(1024)}, bf16[1024,768]{1,0:T(8,128)(2,1)S(1)}, f32[1024,768]{1,0:T(8,128)}) fusion(f32[1024,768]{1,0:T(8,128)S(1)} %fusion.67, f32[768]{0:T(1024)S(1)} %copy-done.48, bf16[1024,768]{1,0:T(8,128)(2,1)S(1)} %copy-done.28, bf16[768,768]{1,0:T(8,128)(2,1)S(1)} %copy-done), kind=kOutput, calls=%fused_computation.20 | convolution fusion | flops 1266941184 | bytes 10622976 | tf_op jit(solution)/shard_map/rd,fd->rf/dot_general | solution.py:134
  130.4 1.2 copy-done.66
  131.6 2.6 convolution_convert_fusion
  134.3 3.3 multiply_convert_fusion.2
  138.7 2.6 convolution_convert_fusion.1
  141.3 1.4 convert_element_type.174
  142.7 19.7 %reduce-scatter.9.cloned.1.call-done = bf16[256,768]{1,0:T(8,128)(2,1)} async-done(((bf16[1024,768]{1,0:T(8,128)(2,1)}), bf16[256,768]{1,0:T(8,128)(2,1)}) %reduce-scatter.9.cloned.1.call-update) | async-done | bytes 393232 | tf_op jit(solution)/shard_map/reduce_scatter | solution.py:141
  162.4 2.1 fusion.47
  164.5 1.2 multiply_multiply_fusion.6
  165.7 27.1 %reduce-scatter.7.cloned.1.call-done = bf16[256,768]{1,0:T(8,128)(2,1)} async-done(((bf16[1024,768]{1,0:T(8,128)(2,1)}), bf16[256,768]{1,0:T(8,128)(2,1)}) %reduce-scatter.7.cloned.1.call-update) | async-done | bytes 393232 | tf_op jit(solution)/shard_map/reduce_scatter | solution.py:105
  192.8 2.6 fusion.59
  195.4 2.4 fusion.36
  199.5 18.1 %all-gather.8.cloned.1.call-done = bf16[1024,768]{1,0:T(8,128)(2,1)} async-done(((bf16[256,768]{1,0:T(8,128)(2,1)}), bf16[1024,768]{1,0:T(8,128)(2,1)}) %all-gather.8.cloned.1.call-update) | async-done | bytes 1572880 | tf_op jit(solution)/shard_map/all_gather | solution.py:154
  217.6 2.1 convolution_convert_fusion.3
  219.8 3.9 multiply_reduce_fusion.1
  224.5 1.4 multiply_convert_fusion.1
  227.7 1.2 fusion.5
  228.8 1.9 multiply_reduce_fusion
  230.8 1.8 convert_reduce_fusion.4
  232.6 1.4 multiply_convert_fusion
  238.2 1.8 add_convert_fusion
  240.4 4.9 fusion.72
  245.3 2.8 fusion.71
  248.1 1.3 fusion.50
  249.4 1.3 fusion.75
  250.7 1.3 fusion.73
  252.0 1.3 fusion.74
  254.2 22.2 %all-reduce.1 = (f32[192]{0:T(256)}, f32[192]{0:T(256)}, f32[768]{0:T(1024)}) all-reduce(f32[192]{0:T(256)S(1)} %reduce_sum.217, f32[192]{0:T(256)S(1)} %reduce_sum.219, f32[768]{0:T(1024)S(1)} %copy-done.62), channel_id=1, replica_groups=mesh['dp'=8,'mp'=4] {'dp'}, use_global_device_ids=true, to_apply=%region_24.25 | all-reduce | flops 1152 | bytes 9216 | tf_op jit(solution)/shard_map/psum | solution.py:228
  276.4 1.3 convert_reduce_fusion.1
  277.7 1.5 fusion.48
  279.2 41.7 %all-reduce = (f32[768]{0:T(1024)}, f32[768]{0:T(1024)}, f32[768]{0:T(1024)}, f32[768]{0:T(1024)}, f32[768]{0:T(1024)}, /*index=5*/f32[768]{0:T(1024)}) all-reduce(f32[768]{0:T(1024)S(1)} %get-tuple-element.19, f32[768]{0:T(1024)S(1)} %get-tuple-element.24, f32[768]{0:T(1024)S(1)} %copy-done.54, ...), channel_id=1, replica_groups=mesh['dp'=8,'mp'=4] {'dp','mp'}, use_global_device_ids=true, to_apply=%region_19.20 | all-reduce | flops 4608 | bytes 36864 | tf_op jit(solution)/shard_map/psum | solution.py:243
  321.0 2.3 add_add_fusion.2
  323.2 184.2 %all-reduce.5.cloned.1.call-done = (f32[768,192]{0,1:T(8,128)}, f32[768,192]{0,1:T(8,128)}, f32[768,192]{0,1:T(8,128)}, f32[192,768]{1,0:T(8,128)}, f32[768,768]{1,0:T(8,128)}, /*index=5*/f32[768,768]{1,0:T(8,128)}) async-done(((f32[768,192]{0,1:T(8,128)}, f32[768,192]{0,1:T(8,128)}, f32[768,192]{0,1:T(8,128)}, f32[192,768]{1,0:T(8,128)}, f32[768,768]{1,0:T(8,128)}, /*index=5*/f32[768,768]{1,0:T(8,128)}), ...) | async-done | bytes 7077904 | tf_op jit(solution)/shard_map/psum | solution.py:228
  507.5 2.1 copy.46
  509.5 1.9 copy.47
  511.5 1.9 copy.48
  514.2 1.4 copy.50
  515.6 1.4 copy.51
  (201 shorter events, 26.8 us)
Async XLA Ops:
  7.2 112.9 %copy-start = (bf16[768,768]{1,0:T(8,128)(2,1)S(1)}, bf16[768,768]{1,0:T(8,128)(2,1)}, u32[]{:S(2)}) copy-start(bf16[768,768]{1,0:T(8,128)(2,1)} %param.35) | copy-start | bytes 3538948
  7.2 29.0 %all-gather.4.cloned.1.call-start = ((), (), s32[]{:S(2)}) async-start(), calls=%async_computation.4 | async-start | bytes 1966080 | tf_op jit(solution)/shard_map/all_gather | solution.py:64
  8.5 5.9 %copy-start.43 = (f32[256]{0:T(256)}, f32[256]{0:T(256)S(1)}, u32[]{:S(2)}) copy-start(f32[256]{0:T(256)S(1)} %broadcast_multiply_fusion.1) | copy-start | bytes 3076
  10.3 4.1 copy-start.49
  11.0 3.4 copy-start.40
  13.7 68.3 %reduce-scatter.5.cloned.1.call-start = ((), (), s32[]{:S(2)}) async-start(), calls=%async_computation.5 | async-start | bytes 1966080 | tf_op jit(solution)/shard_map/reduce_scatter | solution.py:94
  15.1 23.4 %copy-start.37 = (bf16[768,192]{0,1:T(8,128)(2,1)S(1)}, bf16[768,192]{0,1:T(8,128)(2,1)}, u32[]{:S(2)}) copy-start(bf16[768,192]{0,1:T(8,128)(2,1)} %param.26) | copy-start | bytes 884740
  36.2 2.3 copy-start.5
  36.2 3.0 copy-start.20
  38.5 2.1 copy-start.21
  38.5 6.5 %copy-start.17 = (bf16[512,192]{0,1:T(8,128)(2,1)}, bf16[512,192]{0,1:T(8,128)(2,1)S(1)}, u32[]{:S(2)}) copy-start(bf16[512,192]{0,1:T(8,128)(2,1)S(1)} %get-tuple-element.57) | copy-start | bytes 589828
  39.2 5.8 %copy-start.7 = (bf16[1024,192]{0,1:T(8,128)(2,1)}, bf16[1024,192]{0,1:T(8,128)(2,1)S(1)}, u32[]{:S(2)}) copy-start(bf16[1024,192]{0,1:T(8,128)(2,1)S(1)} %convolution_convert_fusion.4) | copy-start | bytes 1179652
  40.7 2.6 copy-start.2
  42.2 2.8 copy-start.45
  42.9 5.1 copy-start.23
  45.0 6.4 %copy-start.29 = (bf16[3,64,512]{2,1,0:T(8,128)(2,1)}, bf16[3,64,512]{2,1,0:T(8,128)(2,1)S(1)}, u32[]{:S(2)}) copy-start(bf16[3,64,512]{2,1,0:T(8,128)(2,1)S(1)} %fusion.35) | copy-start | bytes 589828
  46.4 2.6 copy-start.3
  46.4 2.6 copy-start.42
  49.7 2.3 copy-start.34
  51.3 3.3 copy-start.63
  51.3 30.6 %copy-start.4 = (bf16[256,768]{1,0:T(8,128)(2,1)S(1)}, bf16[256,768]{1,0:T(8,128)(2,1)}, u32[]{:S(2)}) copy-start(bf16[256,768]{1,0:T(8,128)(2,1)} %param.19) | copy-start | bytes 1179652
  53.8 34.2 %copy-start.11 = (bf16[256,768]{1,0:T(8,128)(2,1)S(1)}, bf16[256,768]{1,0:T(8,128)(2,1)}, u32[]{:S(2)}) copy-start(bf16[256,768]{1,0:T(8,128)(2,1)} %param.37) | copy-start | bytes 1179652
  53.8 63.0 %all-gather.6.cloned.1.call-start = ((), (), s32[]{:S(2)}) async-start(), calls=%async_computation.6 | async-start | bytes 1966080 | tf_op jit(solution)/shard_map/all_gather | solution.py:102
  83.2 1.9 copy-start.47
  87.8 74.6 %reduce-scatter.9.cloned.1.call-start = ((), (), s32[]{:S(2)}) async-start(), calls=%async_computation.8 | async-start | bytes 1966080 | tf_op jit(solution)/shard_map/reduce_scatter | solution.py:141
  90.7 14.9 %collective-permute-start = (bf16[256,768]{1,0:T(8,128)(2,1)}, bf16[256,768]{1,0:T(8,128)(2,1)S(1)}, u32[]{:S(2)}, u32[]{:S(2)}) collective-permute-start(bf16[256,768]{1,0:T(8,128)(2,1)} %get-tuple-element.49), channel_id=1, source_target_pairs={{0,1},{1,2},{2,3},{3,0},{4,5},{5,6},{6,7},{7,4},{8,9},{9,10},{10,1... | collective-permute-start | bytes 1179656 | tf_op jit(solution)/shard_map/ppermute | solution.py:124
  90.7 17.2 %collective-permute-start.1 = (bf16[256,768]{1,0:T(8,128)(2,1)}, bf16[256,768]{1,0:T(8,128)(2,1)}, u32[]{:S(2)}, u32[]{:S(2)}) collective-permute-start(bf16[256,768]{1,0:T(8,128)(2,1)} %get-tuple-element.49), channel_id=1, source_target_pairs={{0,3},{1,0},{2,1},{3,2},{4,7},{5,4},{6,5},{7,6},{8,11},{9,8},{10,9... | collective-permute-start | bytes 1179656 | tf_op jit(solution)/shard_map/ppermute | solution.py:129
  105.6 9.4 %collective-permute-start.2 = (bf16[256,768]{1,0:T(8,128)(2,1)S(1)}, bf16[256,768]{1,0:T(8,128)(2,1)}, u32[]{:S(2)}, u32[]{:S(2)}) collective-permute-start(bf16[256,768]{1,0:T(8,128)(2,1)S(1)} %collective-permute-done), channel_id=1, source_target_pairs={{0,1},{1,2},{2,3},{3,0},{4,5},{5,6},{6,7},{7,4},{8,9},{9,10},{10,1... | collective-permute-start | bytes 1179656 | tf_op jit(solution)/shard_map/ppermute | solution.py:124
  116.8 3.3 copy-start.48
  116.8 3.3 copy-start.28
  120.1 10.3 %copy-start.14 = (f32[1024,768]{1,0:T(8,128)}, f32[1024,768]{1,0:T(8,128)S(1)}, u32[]{:S(2)}) copy-start(f32[1024,768]{1,0:T(8,128)S(1)} %fusion.67) | copy-start | bytes 9437188
  120.1 11.5 %copy-start.65 = (bf16[768,768]{1,0:T(8,128)(2,1)S(1)}, bf16[768,768]{1,0:T(8,128)(2,1)}, u32[]{:S(2)}) copy-start(bf16[768,768]{1,0:T(8,128)(2,1)} %param.33) | copy-start | bytes 3538948
  134.2 58.6 %reduce-scatter.7.cloned.1.call-start = ((), (), s32[]{:S(2)}) async-start(), calls=%async_computation.7 | async-start | bytes 1966080 | tf_op jit(solution)/shard_map/reduce_scatter | solution.py:105
  138.7 23.7 %copy-start.6 = (bf16[256,768]{1,0:T(8,128)(2,1)S(1)}, bf16[256,768]{1,0:T(8,128)(2,1)}, u32[]{:S(2)}) copy-start(bf16[256,768]{1,0:T(8,128)(2,1)} %reduce-scatter.5.cloned.1.call-done) | copy-start | bytes 1179652
  141.3 54.2 %copy-start.12 = (bf16[256,768]{1,0:T(8,128)(2,1)S(1)}, bf16[256,768]{1,0:T(8,128)(2,1)}, u32[]{:S(2)}) copy-start(bf16[256,768]{1,0:T(8,128)(2,1)} %param.37) | copy-start | bytes 1179652
  141.3 76.3 %all-gather.8.cloned.1.call-start = ((), (), s32[]{:S(2)}) async-start(), calls=%async_computation.9 | async-start | bytes 1966080 | tf_op jit(solution)/shard_map/all_gather | solution.py:154
  195.4 24.3 %copy-start.24 = (bf16[1024,192]{0,1:T(8,128)(2,1)S(1)}, bf16[1024,192]{0,1:T(8,128)(2,1)}, u32[]{:S(2)}) copy-start(bf16[1024,192]{0,1:T(8,128)(2,1)} %copy-done.23) | copy-start | bytes 1179652
  195.4 2.4 copy-start.56
  197.8 78.5 %reduce-scatter.11.cloned.1.call-start = ((), (), s32[]{:S(2)}) async-start(), calls=%async_computation.10 | async-start | bytes 1966080 | tf_op jit(solution)/shard_map/reduce_scatter | solution.py:206
  219.7 4.0 slice-start
  219.7 4.7 slice-start.1
  223.7 3.9 slice-start.2
  224.5 3.2 slice-start.3
  240.0 267.4 %all-reduce.5.cloned.1.call-start = ((), (), s32[]{:S(2)}) async-start(), calls=%async_computation.11 | async-start | bytes 14155776 | tf_op jit(solution)/shard_map/psum | solution.py:228
  240.3 4.9 copy-start.64
  240.4 4.9 copy-start.67
  245.3 2.9 copy-start.26
  245.3 2.9 copy-start.30
  245.3 2.9 copy-start.32
  248.1 2.6 copy-start.10
  253.3 23.0 %copy-start.41 = (f32[768]{0:T(1024)S(1)}, f32[768]{0:T(1024)}, u32[]{:S(2)}) copy-start(f32[768]{0:T(1024)} %copy-done.40) | copy-start | bytes 9220
  253.3 23.0 %copy-start.44 = (f32[256]{0:T(256)S(1)}, f32[256]{0:T(256)}, u32[]{:S(2)}) copy-start(f32[256]{0:T(256)} %copy-done.43) | copy-start | bytes 3076
  253.3 24.3 %copy-start.59 = (f32[256]{0:T(256)S(1)}, f32[256]{0:T(256)}, u32[]{:S(2)}) copy-start(f32[256]{0:T(256)} %copy-done.58) | copy-start | bytes 3076
  253.3 24.4 %copy-start.50 = (f32[256]{0:T(256)S(1)}, f32[256]{0:T(256)}, u32[]{:S(2)}) copy-start(f32[256]{0:T(256)} %copy-done.49) | copy-start | bytes 3076
  253.4 25.8 %copy-start.51 = (f32[768]{0:T(1024)S(1)}, f32[768]{0:T(1024)}, u32[]{:S(2)}) copy-start(f32[768]{0:T(1024)} %get-tuple-element.17) | copy-start | bytes 9220
  253.4 25.8 %copy-start.52 = (f32[768]{0:T(1024)S(1)}, f32[768]{0:T(1024)}, u32[]{:S(2)}) copy-start(f32[768]{0:T(1024)} %get-tuple-element.23) | copy-start | bytes 9220
  253.4 25.8 %copy-start.53 = (f32[768]{0:T(1024)S(1)}, f32[768]{0:T(1024)}, u32[]{:S(2)}) copy-start(f32[768]{0:T(1024)} %get-tuple-element.21) | copy-start | bytes 9220
  253.4 25.8 %copy-start.54 = (f32[768]{0:T(1024)S(1)}, f32[768]{0:T(1024)}, u32[]{:S(2)}) copy-start(f32[768]{0:T(1024)} %get-tuple-element.22) | copy-start | bytes 9220
  253.4 67.6 %copy-start.13 = (bf16[256,768]{1,0:T(8,128)(2,1)S(1)}, bf16[256,768]{1,0:T(8,128)(2,1)}, u32[]{:S(2)}) copy-start(bf16[256,768]{1,0:T(8,128)(2,1)} %param.37) | copy-start | bytes 1179652
  253.4 67.5 %copy-start.57 = (f32[256]{0:T(256)S(1)}, f32[256]{0:T(256)}, u32[]{:S(2)}) copy-start(f32[256]{0:T(256)} %copy-done.56) | copy-start | bytes 3076
  507.5 5.9 %copy-start.33 = (f32[192,768]{1,0:T(8,128)S(1)}, f32[192,768]{1,0:T(8,128)}, u32[]{:S(2)}) copy-start(f32[192,768]{1,0:T(8,128)} %get-tuple-element.79) | copy-start | bytes 1769476
  507.5 6.7 %copy-start.16 = (f32[768,768]{1,0:T(8,128)S(1)}, f32[768,768]{1,0:T(8,128)}, u32[]{:S(2)}) copy-start(f32[768,768]{1,0:T(8,128)} %get-tuple-element.83) | copy-start | bytes 7077892
  513.4 2.2 copy-start.15
  514.2 2.8 copy-start.1
  (19 other events, 19.8 us)
Sparse Core Ops, SparseCore 0:
  13.8 22.3 all-gather.3
  53.9 27.9 reduce-scatter.4
  87.9 25.2 all-gather.5
  134.3 28.0 reduce-scatter.8
  164.8 27.9 reduce-scatter.6
  197.9 19.6 all-gather.7
  240.2 28.0 reduce-scatter.10
  274.4 232.9 all-reduce.4
